TPU v7x, 32 devices: a whole 2x2x4 slice. The times are simulated.
32 devices in a mesh: dp: 8 (over y, x, core), fsdp: 4 (over z).
Axes of the slice: x: 2, y: 2, z: 4, core: 2. Of those that a mesh axis runs over, the one named last changes fastest.
Arguments:
- tokens: bfloat16 [32768, 768], P(('dp', 'fsdp')), may hold values from -6 to 6
- cotangent: bfloat16 [32768, 768], P(('dp', 'fsdp')), may hold values from -6 to 6
- doc_lengths: int32 [64, 4], P(('dp', 'fsdp')), may hold values from 1 to 288, 512 in all within a row
- query_ids: int32 [256, 1], P(('dp', 'fsdp')), may hold values from 0 to 63
- qkv_weight: bfloat16 [768, 2304], P(('dp', 'fsdp')), may hold values from -0.21875 to 0.21875
- query_bias: bfloat16 [768], P(('dp', 'fsdp')), may hold values from -3 to 3
- value_bias: bfloat16 [768], P(('dp', 'fsdp')), may hold values from -3 to 3
- attn_weight: bfloat16 [768, 768], P(('dp', 'fsdp')), may hold values from -0.875 to 0.875
- attn_bias: bfloat16 [768], P(('dp', 'fsdp')), may hold values from -2 to 2
- first_gain: bfloat16 [768], P(('dp', 'fsdp')), may hold values from 0.5 to 1.5
- first_shift: bfloat16 [768], P(('dp', 'fsdp')), may hold values from -2 to 2
- inner_weight: bfloat16 [768, 3072], P(('dp', 'fsdp')), may hold values from -0.21875 to 0.21875
- inner_bias: bfloat16 [3072], P(('dp', 'fsdp')), may hold values from -3 to 3
- outer_weight: bfloat16 [3072, 768], P(('dp', 'fsdp')), may hold values from -0.21875 to 0.21875
- outer_bias: bfloat16 [768], P(('dp', 'fsdp')), may hold values from -2 to 2
- second_gain: bfloat16 [768], P(('dp', 'fsdp')), may hold values from 0.5 to 1.5
- second_shift: bfloat16 [768], P(('dp', 'fsdp')), may hold values from -2 to 2
- span_weight: bfloat16 [768, 128], P(('dp', 'fsdp')), may hold values from -0.21875 to 0.21875
- answer_vector: bfloat16 [128], P(('dp', 'fsdp')), may hold values from -1 to 1
Outputs:
- log_likelihood: float32 [], replicated
- layer_output: bfloat16 [32768, 768], P(('dp', 'fsdp'))
- input_grad: float32 [32768, 768], P(('dp', 'fsdp'))
- qkv_weight_grad: float32 [768, 2304], P(('dp', 'fsdp'))
- query_bias_grad: float32 [768], P(('dp', 'fsdp'))
- value_bias_grad: float32 [768], P(('dp', 'fsdp'))
- attn_weight_grad: float32 [768, 768], P(('dp', 'fsdp'))
- attn_bias_grad: float32 [768], P(('dp', 'fsdp'))
- first_gain_grad: float32 [768], P(('dp', 'fsdp'))
- first_shift_grad: float32 [768], P(('dp', 'fsdp'))
- inner_weight_grad: float32 [768, 3072], P(('dp', 'fsdp'))
- inner_bias_grad: float32 [3072], P(('dp', 'fsdp'))
- outer_weight_grad: float32 [3072, 768], P(('dp', 'fsdp'))
- outer_bias_grad: float32 [768], P(('dp', 'fsdp'))
- second_gain_grad: float32 [768], P(('dp', 'fsdp'))
- second_shift_grad: float32 [768], P(('dp', 'fsdp'))
- span_weight_grad: float32 [768, 128], P(('dp', 'fsdp'))
- answer_vector_grad: float32 [128], P(('dp', 'fsdp'))
Inputs may be any that keep to these rules, and one draw needn't show every extreme that they name: `doc_lengths`: the 4 lengths of a pack sum to 512, and in every pack one of them is 288. `query_ids`: every query has one segment or more.
All inputs are finite; a program needn't handle non-finite values.
Results may differ from a plain program's by a relative error of at most 0.014.
Values may be sent and summed in bfloat16 or wider, within the bound.
No kernel may reach another device: no remote copies, remote signals or barrier semaphores. Data moves between devices by JAX's collectives and lax.ppermute only.
A program may use at most 192 MiB of HBM per device.

v0:
```python
import math
import jax
import jax.numpy as jnp
from jax import lax
from jax.sharding import PartitionSpec as P

HEADS = 12
HEAD_DIM = 64
PACK = 512
SEGS_PACK = 4
HIGHEST = lax.Precision.HIGHEST
MASKED = -1e30


def matmul(operand, matrix):
    return jnp.dot(operand, matrix, preferred_element_type=jnp.float32)


def weight_grad(operand, matrix):
    return lax.dot_general(
        operand, matrix, (((0,), (0,)), ((), ())), preferred_element_type=jnp.float32
    )


def back_prod(operand, matrix):
    return lax.dot_general(
        operand, matrix, (((1,), (1,)), ((), ())), preferred_element_type=jnp.float32
    )


def normalize(hidden):
    center = hidden - jnp.mean(hidden, axis=-1, keepdims=True)
    factor = lax.rsqrt(jnp.mean(center * center, axis=-1, keepdims=True) + 1e-06)
    return (center * factor, factor)


def norm_back(gradient, normed, factor):
    return factor * (
        gradient
        - jnp.mean(gradient, axis=-1, keepdims=True)
        - normed * jnp.mean(gradient * normed, axis=-1, keepdims=True)
    )


def segment_ids(lengths):
    bounds = jnp.cumsum(lengths, axis=1)
    places = lax.broadcasted_iota(jnp.int32, (1, PACK, 1), 1)
    return jnp.sum((places >= bounds[:, None, :]).astype(jnp.int32), axis=-1)


def exact_gelu(inner_pre):
    return jax.nn.gelu(inner_pre, approximate=False)


def masked_scores(query_heads, key_heads, segment):
    scaling = 1.0 / math.sqrt(query_heads.shape[-1])
    same_segment = segment[:, None] == segment[None, :]
    raw_scores = (
        jnp.einsum("qhd,khd->hqk", query_heads, key_heads, preferred_element_type=jnp.float32)
        * scaling
    )
    return jnp.where(same_segment[None], raw_scores, MASKED)


def attend(pieces):
    query_heads, key_heads, value_heads, segment = pieces
    scores = masked_scores(query_heads, key_heads, segment)
    highest = jnp.max(scores, axis=-1, keepdims=True)
    weights = jnp.exp(scores - highest)
    totals = jnp.sum(weights, axis=-1, keepdims=True)
    shares = (weights / totals).astype(jnp.bfloat16)
    context = jnp.einsum("hqk,khd->qhd", shares, value_heads, preferred_element_type=jnp.float32)
    return (context.astype(jnp.bfloat16), highest + jnp.log(totals))


def attend_back(pieces):
    query_heads, key_heads, value_heads, segment, logsum, context_grad = pieces
    scaling = 1.0 / math.sqrt(query_heads.shape[-1])
    scores = masked_scores(query_heads, key_heads, segment)
    softmax = jnp.exp(scores - logsum)
    value_grad = jnp.einsum(
        "hqk,qhd->khd",
        softmax.astype(jnp.bfloat16),
        context_grad,
        preferred_element_type=jnp.float32,
    )
    shares_grad = jnp.einsum(
        "qhd,khd->hqk", context_grad, value_heads, preferred_element_type=jnp.float32
    )
    score_grad = softmax * (shares_grad - jnp.sum(softmax * shares_grad, axis=-1, keepdims=True))
    score_low = score_grad.astype(jnp.bfloat16)
    query_grad = (
        jnp.einsum("hqk,khd->qhd", score_low, key_heads, preferred_element_type=jnp.float32)
        * scaling
    )
    key_grad = (
        jnp.einsum("hqk,qhd->khd", score_low, query_heads, preferred_element_type=jnp.float32)
        * scaling
    )
    stacked = jnp.stack([query_grad, key_grad, value_grad], axis=1)
    return stacked.reshape(stacked.shape[0], -1)


def shards(
    tokens,
    cotangent,
    doc_lengths,
    query_ids,
    qkv_weight,
    query_bias,
    value_bias,
    attn_weight,
    attn_bias,
    first_gain,
    first_shift,
    inner_weight,
    inner_bias,
    outer_weight,
    outer_bias,
    second_gain,
    second_shift,
    span_weight,
    answer_vector,
):
    rows_here = tokens.shape[0]
    width = tokens.shape[1]
    packs_here = rows_here // PACK
    gathered = (
        lax.all_gather(qkv_weight, ("dp", "fsdp"), axis=0, tiled=True),
        lax.all_gather(query_bias, ("dp", "fsdp"), axis=0, tiled=True),
        lax.all_gather(value_bias, ("dp", "fsdp"), axis=0, tiled=True),
        lax.all_gather(attn_weight, ("dp", "fsdp"), axis=0, tiled=True),
        lax.all_gather(attn_bias, ("dp", "fsdp"), axis=0, tiled=True),
        lax.all_gather(first_gain, ("dp", "fsdp"), axis=0, tiled=True),
        lax.all_gather(first_shift, ("dp", "fsdp"), axis=0, tiled=True),
        lax.all_gather(inner_weight, ("dp", "fsdp"), axis=0, tiled=True),
        lax.all_gather(inner_bias, ("dp", "fsdp"), axis=0, tiled=True),
        lax.all_gather(outer_weight, ("dp", "fsdp"), axis=0, tiled=True),
        lax.all_gather(outer_bias, ("dp", "fsdp"), axis=0, tiled=True),
        lax.all_gather(second_gain, ("dp", "fsdp"), axis=0, tiled=True),
        lax.all_gather(second_shift, ("dp", "fsdp"), axis=0, tiled=True),
        lax.all_gather(span_weight, ("dp", "fsdp"), axis=0, tiled=True),
        lax.all_gather(answer_vector, ("dp", "fsdp"), axis=0, tiled=True),
    )
    (
        mix_full,
        query_add,
        value_add,
        attn_full,
        attn_add,
        gain_one,
        shift_one,
        inner_full,
        inner_add,
        outer_full,
        outer_add,
        gain_two,
        shift_two,
        span_full,
        answer_full,
    ) = gathered
    segment = segment_ids(doc_lengths)
    qkv_add = jnp.concatenate([query_add, jnp.zeros_like(query_add), value_add]).astype(jnp.float32)
    mixed_rows = (matmul(tokens, mix_full) + qkv_add).astype(jnp.bfloat16)
    head_split = mixed_rows.reshape(packs_here, PACK, 3, HEADS, HEAD_DIM)
    query_heads = head_split[:, :, 0]
    key_heads = head_split[:, :, 1]
    value_heads = head_split[:, :, 2]
    context, logsum = lax.map(attend, (query_heads, key_heads, value_heads, segment))
    context = context.reshape(rows_here, width)
    attended = matmul(context, attn_full) + attn_add.astype(jnp.float32)
    normed_one, factor_one = normalize(tokens.astype(jnp.float32) + attended)
    first_norm = normed_one * gain_one.astype(jnp.float32) + shift_one.astype(jnp.float32)
    first_low = first_norm.astype(jnp.bfloat16)
    inner_pre = matmul(first_low, inner_full) + inner_add.astype(jnp.float32)
    active, gelu_back = jax.vjp(exact_gelu, inner_pre)
    active_low = active.astype(jnp.bfloat16)
    outer_out = matmul(active_low, outer_full) + outer_add.astype(jnp.float32)
    normed_two, factor_two = normalize(first_norm + outer_out)
    result = (normed_two * gain_two.astype(jnp.float32) + shift_two.astype(jnp.float32)).astype(
        jnp.bfloat16
    )
    span_rows = matmul(result, span_full)
    answer_wide = answer_full.astype(jnp.float32)
    token_score = jnp.dot(span_rows, answer_wide, precision=HIGHEST).reshape(packs_here, PACK)
    member = segment[:, None, :] == lax.broadcasted_iota(jnp.int32, (1, SEGS_PACK, 1), 1)
    doc_score = jax.nn.logsumexp(jnp.where(member, token_score[:, None, :], MASKED), axis=-1)
    doc_flat = doc_score.reshape(-1)
    queries_all = packs_here * lax.axis_size("dp") * lax.axis_size("fsdp")
    member_query = query_ids == lax.broadcasted_iota(jnp.int32, (1, queries_all), 1)
    local_peak = jnp.max(jnp.where(member_query, doc_flat[:, None], MASKED), axis=0)
    local_mass = jnp.sum(
        jnp.where(member_query, jnp.exp(doc_flat[:, None] - local_peak[None, :]), 0.0), axis=0
    )
    peak_score = lax.pmax(local_peak, ("dp", "fsdp"))
    mass_total = lax.psum(local_mass * jnp.exp(local_peak - peak_score), ("dp", "fsdp"))
    marginal = peak_score + jnp.log(mass_total)
    likelihood = jnp.sum(marginal)
    gathered = (
        lax.all_gather(qkv_weight, ("dp", "fsdp"), axis=0, tiled=True),
        lax.all_gather(query_bias, ("dp", "fsdp"), axis=0, tiled=True),
        lax.all_gather(value_bias, ("dp", "fsdp"), axis=0, tiled=True),
        lax.all_gather(attn_weight, ("dp", "fsdp"), axis=0, tiled=True),
        lax.all_gather(attn_bias, ("dp", "fsdp"), axis=0, tiled=True),
        lax.all_gather(first_gain, ("dp", "fsdp"), axis=0, tiled=True),
        lax.all_gather(first_shift, ("dp", "fsdp"), axis=0, tiled=True),
        lax.all_gather(inner_weight, ("dp", "fsdp"), axis=0, tiled=True),
        lax.all_gather(inner_bias, ("dp", "fsdp"), axis=0, tiled=True),
        lax.all_gather(outer_weight, ("dp", "fsdp"), axis=0, tiled=True),
        lax.all_gather(outer_bias, ("dp", "fsdp"), axis=0, tiled=True),
        lax.all_gather(second_gain, ("dp", "fsdp"), axis=0, tiled=True),
        lax.all_gather(second_shift, ("dp", "fsdp"), axis=0, tiled=True),
        lax.all_gather(span_weight, ("dp", "fsdp"), axis=0, tiled=True),
        lax.all_gather(answer_vector, ("dp", "fsdp"), axis=0, tiled=True),
    )
    (
        mix_full,
        query_add,
        value_add,
        attn_full,
        attn_add,
        gain_one,
        shift_one,
        inner_full,
        inner_add,
        outer_full,
        outer_add,
        gain_two,
        shift_two,
        span_full,
        answer_full,
    ) = gathered
    seg_marginal = jnp.sum(jnp.where(member_query, marginal[None, :], 0.0), axis=1).reshape(
        packs_here, SEGS_PACK
    )
    doc_weight = jnp.exp(doc_score - seg_marginal)
    token_weight = jnp.sum(
        jnp.where(
            member,
            doc_weight[:, :, None] * jnp.exp(token_score[:, None, :] - doc_score[:, :, None]),
            0.0,
        ),
        axis=1,
    ).reshape(rows_here)
    answer_grad = jnp.dot(token_weight, span_rows, precision=HIGHEST)
    span_grad = (token_weight[:, None] * answer_full.astype(jnp.float32)[None, :]).astype(
        jnp.bfloat16
    )
    span_weight_grad = weight_grad(result, span_grad)
    result_grad = cotangent.astype(jnp.float32) + back_prod(span_grad, span_full)
    second_gain_grad = jnp.sum(result_grad * normed_two, axis=0)
    second_shift_grad = jnp.sum(result_grad, axis=0)
    second_sum_grad = norm_back(result_grad * gain_two.astype(jnp.float32), normed_two, factor_two)
    outer_low = second_sum_grad.astype(jnp.bfloat16)
    outer_weight_grad = weight_grad(active_low, outer_low)
    outer_bias_grad = jnp.sum(outer_low.astype(jnp.float32), axis=0)
    (inner_grad,) = gelu_back(back_prod(outer_low, outer_full))
    inner_low = inner_grad.astype(jnp.bfloat16)
    inner_weight_grad = weight_grad(first_low, inner_low)
    inner_bias_grad = jnp.sum(inner_low.astype(jnp.float32), axis=0)
    first_grad = second_sum_grad + back_prod(inner_low, inner_full)
    first_gain_grad = jnp.sum(first_grad * normed_one, axis=0)
    first_shift_grad = jnp.sum(first_grad, axis=0)
    first_sum_grad = norm_back(first_grad * gain_one.astype(jnp.float32), normed_one, factor_one)
    attended_low = first_sum_grad.astype(jnp.bfloat16)
    attn_weight_grad = weight_grad(context, attended_low)
    attn_bias_grad = jnp.sum(attended_low.astype(jnp.float32), axis=0)
    context_grad = back_prod(attended_low, attn_full).astype(jnp.bfloat16)
    context_grad = context_grad.reshape(packs_here, PACK, HEADS, HEAD_DIM)
    mixed_grad = lax.map(
        attend_back, (query_heads, key_heads, value_heads, segment, logsum, context_grad)
    )
    mixed_low = mixed_grad.reshape(rows_here, 3 * width).astype(jnp.bfloat16)
    qkv_weight_grad = weight_grad(tokens, mixed_low)
    bias_sums = jnp.sum(mixed_low.astype(jnp.float32), axis=0)
    query_bias_grad = bias_sums[:width]
    value_bias_grad = bias_sums[2 * width :]
    input_grad = back_prod(mixed_low, mix_full) + first_sum_grad
    owned_grads = (
        lax.psum_scatter(qkv_weight_grad, ("dp", "fsdp"), scatter_dimension=0, tiled=True),
        lax.psum_scatter(query_bias_grad, ("dp", "fsdp"), scatter_dimension=0, tiled=True),
        lax.psum_scatter(value_bias_grad, ("dp", "fsdp"), scatter_dimension=0, tiled=True),
        lax.psum_scatter(attn_weight_grad, ("dp", "fsdp"), scatter_dimension=0, tiled=True),
        lax.psum_scatter(attn_bias_grad, ("dp", "fsdp"), scatter_dimension=0, tiled=True),
        lax.psum_scatter(first_gain_grad, ("dp", "fsdp"), scatter_dimension=0, tiled=True),
        lax.psum_scatter(first_shift_grad, ("dp", "fsdp"), scatter_dimension=0, tiled=True),
        lax.psum_scatter(inner_weight_grad, ("dp", "fsdp"), scatter_dimension=0, tiled=True),
        lax.psum_scatter(inner_bias_grad, ("dp", "fsdp"), scatter_dimension=0, tiled=True),
        lax.psum_scatter(outer_weight_grad, ("dp", "fsdp"), scatter_dimension=0, tiled=True),
        lax.psum_scatter(outer_bias_grad, ("dp", "fsdp"), scatter_dimension=0, tiled=True),
        lax.psum_scatter(second_gain_grad, ("dp", "fsdp"), scatter_dimension=0, tiled=True),
        lax.psum_scatter(second_shift_grad, ("dp", "fsdp"), scatter_dimension=0, tiled=True),
        lax.psum_scatter(span_weight_grad, ("dp", "fsdp"), scatter_dimension=0, tiled=True),
        lax.psum_scatter(answer_grad, ("dp", "fsdp"), scatter_dimension=0, tiled=True),
    )
    return (likelihood, result, input_grad) + tuple(owned_grads)


def solution(mesh):
    in_specs = (
        P(("dp", "fsdp"), None),
        P(("dp", "fsdp"), None),
        P(("dp", "fsdp"), None),
        P(("dp", "fsdp"), None),
        P(("dp", "fsdp"), None),
        P(("dp", "fsdp")),
        P(("dp", "fsdp")),
        P(("dp", "fsdp"), None),
        P(("dp", "fsdp")),
        P(("dp", "fsdp")),
        P(("dp", "fsdp")),
        P(("dp", "fsdp"), None),
        P(("dp", "fsdp")),
        P(("dp", "fsdp"), None),
        P(("dp", "fsdp")),
        P(("dp", "fsdp")),
        P(("dp", "fsdp")),
        P(("dp", "fsdp"), None),
        P(("dp", "fsdp")),
    )
    out_specs = (
        P(),
        P(("dp", "fsdp"), None),
        P(("dp", "fsdp"), None),
        P(("dp", "fsdp"), None),
        P(("dp", "fsdp")),
        P(("dp", "fsdp")),
        P(("dp", "fsdp"), None),
        P(("dp", "fsdp")),
        P(("dp", "fsdp")),
        P(("dp", "fsdp")),
        P(("dp", "fsdp"), None),
        P(("dp", "fsdp")),
        P(("dp", "fsdp"), None),
        P(("dp", "fsdp")),
        P(("dp", "fsdp")),
        P(("dp", "fsdp")),
        P(("dp", "fsdp"), None),
        P(("dp", "fsdp")),
    )
    return jax.shard_map(shards, mesh=mesh, in_specs=in_specs, out_specs=out_specs, check_vma=False)
```

profile of v0, /device:TPU:0, one launch (start us, length us, event | category | flops | bytes accessed | tf_op | source)
XLA Modules:
  0.0 978.1 jit_solution(9499859527295209149)
XLA Ops:
  19.5 42.6 %all-reduce.22 = (bf16[768]{0:T(1024)(128)(2,1)S(1)}, bf16[768]{0:T(1024)(128)(2,1)S(1)}, bf16[768]{0:T(1024)(128)(2,1)S(1)}, bf16[768]{0:T(1024)(128)(2,1)S(1)}...) all-reduce(bf16[768]{0:T(1024)(128)(2,1)S(1)} %dynamic-update-slice, ...), channel_id=1, replica_groups=mesh['dp'=8,'fsdp'=4] {'dp','fsdp'}, use_global_device_ids=true, to_apply=%add.1 | all-reduce | flops 9344 | bytes 37376
  62.1 2.6 copy.106
  66.5 72.9 %all_gather.66 = bf16[768,128]{1,0:T(8,128)(2,1)} all-gather(bf16[24,128]{1,0:T(8,128)(2,1)S(1)} %copy-done.34), channel_id=1, replica_groups=mesh['dp'=8,'fsdp'=4] {'dp','fsdp'}, dimensions={0}, use_global_device_ids=true | all-gather | bytes 202752 | tf_op jit(solution)/shard_map/all_gather | solution.py:142
  139.9 1.6 copy.113
  141.6 7.5 add_convert_fusion.1
  149.1 6.6 copy.107
  155.7 8.9 reshape.253
  164.6 5.4 slice_bitcast_fusion
  172.1 20.9 %while.22 = (s32[]{:T(128)}, bf16[2,512,12,64]{1,3,2,0:T(8,128)(2,1)}, f32[2,12,512,1]{2,1,3,0:T(8,128)S(1)}, bf16[2,512,12,64]{1,3,2,0:T(8,128)(2,1)}, s32[2,51...) while((s32[]{:T(128)}, ...), condition=%wide.region_5.6_spmd, body=%wide.region_2.5_spmd.sunk | while | flops 843704320 | bytes 42172508 | solution.py:169
  172.3 2.1 fusion.124
  174.4 2.6 fusion.125
  177.0 5.5 fusion.126
  182.7 2.1 fusion.124
  184.8 2.6 fusion.125
  187.3 5.5 fusion.126
  193.0 4.2 copy.111
  197.2 1.6 copy.159
  198.8 3.9 fusion.79
  202.7 1.6 copy-done.9
  204.8 37.9 %multiply_convert_fusion.1 = (bf16[1024,3072]{1,0:T(8,128)(2,1)}, f32[1024,3072]{1,0:T(8,128)}, f32[1024,3072]{1,0:T(8,128)}) fusion(f32[3072]{0:T(1024)S(1)} %convert_element_type.113, bf16[768,3072]{1,0:T(8,128)(2,1)} %all-gather.9.cloned.1.call-done, f32[1024,768]{0,1:T(8,128)} %copy-done.9, f32[768]{0:T(1024)S(1)} %convert_element_type.111, ...), kind=kOutput, calls=%fused_computation.64 | convolution fusion | flops 5043388416 | bytes 39348224 | tf_op jit(solution)/shard_map/dot_general | solution.py:16
  242.7 17.4 %all-gather.11.cloned.1.call-done = bf16[3072,768]{1,0:T(8,128)(2,1)} async-done(((bf16[96,768]{1,0:T(8,128)(2,1)}), bf16[3072,768]{1,0:T(8,128)(2,1)}) %all-gather.11.cloned.1.call-update) | async-done | bytes 4718608 | tf_op jit(solution)/shard_map/all_gather | solution.py:138
  260.2 9.7 fusion.80
  270.3 1.7 add_convert_fusion.2
  272.0 2.0 fusion.81
  275.8 39.6 %pmax.7 = f32[64]{0:T(128)S(1)} all-reduce(f32[64]{0:T(128)S(1)} %select_reduce_fusion.4), channel_id=1, replica_groups=mesh['dp'=8,'fsdp'=4] {'dp','fsdp'}, use_global_device_ids=true, to_apply=%region_13.14 | all-reduce | flops 64 | bytes 512 | tf_op jit(solution)/shard_map/pmax | solution.py:195
  315.5 39.5 %psum.7 = f32[64]{0:T(128)S(1)} all-reduce(f32[64]{0:T(128)S(1)} %exponential_multiply_fusion), channel_id=1, replica_groups=mesh['dp'=8,'fsdp'=4] {'dp','fsdp'}, use_global_device_ids=true, to_apply=%region_15.16 | all-reduce | flops 64 | bytes 512 | tf_op jit(solution)/shard_map/psum | solution.py:196
  356.0 2.9 fusion.54
  358.9 5.1 multiply_reduce_fusion.1
  364.0 5.2 convert_reduce_fusion.2
  369.2 20.2 %convert_reduce_fusion = (f32[3072]{0:T(1024)}, bf16[1024,3072]{1,0:T(8,128)(2,1)}) fusion(f32[1024,3072]{1,0:T(8,128)} %get-tuple-element.293, bf16[3072,768]{1,0:T(8,128)(2,1)} %all-gather.11.cloned.1.call-done, f32[1024,768]{0,1:T(8,128)} %get-tuple-element.285, f32[1024,3072]{1,0:T(8,128)} %get-tuple-element.305, f32[3072]{0:T(1024)S(1)} %convert_element_type.113), kind=kOutput, calls=%fused_computation.62 | convolution fusion | flops 4886098944 | bytes 39346176 | tf_op jit(solution)/shard_map/dot_general | solution.py:26
  389.4 10.8 %multiply_reduce_fusion.2 = (f32[768]{0:T(1024)}, f32[1024]{0:T(1024)S(1)}, f32[1024]{0:T(1024)S(1)}, f32[768]{0:T(1024)}, f32[1024,768]{0,1:T(8,128)S(1)}) fusion(f32[1024,768]{0,1:T(8,128)S(1)} %copy-done.10, f32[1024]{0:T(1024)S(1)} %add_rsqrt_fusion.1, f32[1024]{0:T(1024)S(1)} %broadcast_multiply_fusion.5, f32[768]{0:T(1024)S(1)} %convert_element_type.110, ...), kind=kOutput, calls=%fused_computation.83 | convolution fusion | flops 4839698432 | bytes 20472832 | tf_op jit(solution)/shard_map/dot_general | solution.py:26
  400.2 1.7 convert_reduce_fusion.3
  401.9 1.6 copy-done.14
  407.1 1.5 copy.119
  408.6 5.4 fusion.64
  414.1 57.4 %while.23 = (s32[]{:T(128)}, bf16[2,512,2304]{2,1,0:T(8,128)(2,1)}, bf16[2,512,12,64]{1,3,2,0:T(8,128)(2,1)S(1)}, s32[2,512]{1,0:T(2,128)S(1)}, bf16[2,512,12,64...) while((s32[]{:T(128)}, bf16[2,512,2304]{2,1,0:T(8,128)(2,1)}, ...), condition=%wide.region_25.26_spmd, body=%wide.region_23.25_spmd.sunk | while | flops 2064640000 | bytes 149095184 | solution.py:270
  414.1 1.8 fusion.135
  416.3 6.9 multiply_reduce_fusion.10
  423.2 7.0 multiply_convert_fusion.6
  431.3 2.0 multiply_bitcast_fusion.4
  433.3 3.2 fusion.136
  436.8 2.6 copy.163
  439.4 3.4 constant_dynamic-update-slice_fusion.2
  442.7 1.8 fusion.135
  444.9 6.9 multiply_reduce_fusion.10
  451.8 7.0 multiply_convert_fusion.6
  459.9 2.0 multiply_bitcast_fusion.4
  461.9 3.2 fusion.136
  465.4 2.6 copy.163
  468.0 3.4 constant_dynamic-update-slice_fusion.2
  471.6 9.7 convolution_bitcast_fusion
  481.3 8.1 copy.134
  489.5 1.9 copy-done.15
  491.3 10.2 %fusion.67 = f32[3072,768]{1,0:T(8,128)} fusion(bf16[1024,3072]{1,0:T(8,128)(2,1)} %get-tuple-element.292, f32[1024,768]{0,1:T(8,128)S(1)} %copy-done.15), kind=kOutput, calls=%fused_computation.147 | convolution fusion | flops 4832624640 | bytes 18874368 | tf_op jit(solution)/shard_map/dot_general | solution.py:20
  501.7 1.8 copy-done.11
  503.5 10.5 %fusion.71 = f32[768,3072]{1,0:T(8,128)} fusion(bf16[1024,3072]{1,0:T(8,128)(2,1)} %get-tuple-element.311, f32[1024,768]{0,1:T(8,128)S(1)} %copy-done.11, f32[768]{0:T(1024)S(1)} %copy-done.40, f32[768]{0:T(1024)S(1)} %copy-done.29, f32[1024]{0:T(1024)S(1)} %copy-done.31, f32[1024]{0:T(1024)S(1)} %copy-done.22), kind=kOutput, calls=%fused_computation.151 | convolution fusion | flops 4835770368 | bytes 18888704 | tf_op jit(solution)/shard_map/dot_general | solution.py:20
  514.1 2.7 copy.123
  517.1 3.1 convert_reduce_fusion.1
  520.3 41.8 %all-reduce.21 = (f32[768]{0:T(1024)S(1)}, f32[768]{0:T(1024)S(1)}, f32[768]{0:T(1024)S(1)}, f32[768]{0:T(1024)S(1)}, f32[768]{0:T(1024)S(1)}, /*index=5*/f32[30...) all-reduce(f32[768]{0:T(1024)S(1)} %get-tuple-element.302, ...), channel_id=3, replica_groups=mesh['dp'=8,'fsdp'=4] {'dp','fsdp'}, use_global_device_ids=true, to_apply=%region_28.29.clone | all-reduce | flops 9344 | bytes 74752
  566.7 8.1 convolution_add_fusion.1
  574.9 2.4 copy.124
  578.4 109.4 %reduce-scatter.16.cloned.1.call-done = f32[24,2304]{1,0:T(8,128)} async-done(((f32[768,2304]{1,0:T(8,128)}), f32[24,2304]{1,0:T(8,128)}) %reduce-scatter.16.cloned.1.call-update) | async-done | bytes 221200
  687.9 142.5 %reduce-scatter.14.cloned.1.call-done = f32[96,768]{1,0:T(8,128)} async-done(((f32[3072,768]{1,0:T(8,128)}), f32[96,768]{1,0:T(8,128)}) %reduce-scatter.14.cloned.1.call-update) | async-done | bytes 294928 | tf_op jit(solution)/shard_map/reduce_scatter | solution.py:289
  830.3 141.0 %reduce-scatter.12.cloned.1.call-done = f32[24,3072]{1,0:T(8,128)} async-done(((f32[768,3072]{1,0:T(8,128)}), f32[24,3072]{1,0:T(8,128)}) %reduce-scatter.12.cloned.1.call-update) | async-done | bytes 294928 | tf_op jit(solution)/shard_map/reduce_scatter | solution.py:287
  (220 shorter events, 34.1 us)
Async XLA Ops:
  7.2 59.3 %copy-start.34 = (bf16[24,128]{1,0:T(8,128)(2,1)S(1)}, bf16[24,128]{1,0:T(8,128)(2,1)}, u32[]{:S(2)}) copy-start(bf16[24,128]{1,0:T(8,128)(2,1)} %param.40) | copy-start | bytes 18436
  7.2 132.7 %copy-start.16 = (bf16[1024,768]{1,0:T(8,128)(2,1)S(1)}, bf16[1024,768]{1,0:T(8,128)(2,1)}, u32[]{:S(2)}) copy-start(bf16[1024,768]{1,0:T(8,128)(2,1)} %param.24) | copy-start | bytes 4718596
  7.2 134.3 %all-gather.5.cloned.1.call-start = ((), (), s32[]{:S(2)}) async-start(), calls=%async_computation.5 | async-start | bytes 3649536 | tf_op jit(solution)/shard_map/all_gather | solution.py:129
  7.9 133.6 %copy-start.17 = (bf16[1024,768]{1,0:T(8,128)(2,1)S(1)}, bf16[1024,768]{1,0:T(8,128)(2,1)}, u32[]{:S(2)}) copy-start(bf16[1024,768]{1,0:T(8,128)(2,1)} %param.23) | copy-start | bytes 4718596
  8.0 190.8 %all-gather.7.cloned.1.call-start = ((), (), s32[]{:S(2)}) async-start(), calls=%async_computation.6 | async-start | bytes 1216512 | tf_op jit(solution)/shard_map/all_gather | solution.py:132
  8.7 196.1 %all-gather.9.cloned.1.call-start = ((), (), s32[]{:S(2)}) async-start(), calls=%async_computation.7 | async-start | bytes 4866048 | tf_op jit(solution)/shard_map/all_gather | solution.py:136
  9.4 250.7 %all-gather.11.cloned.1.call-start = ((), (), s32[]{:S(2)}) async-start(), calls=%async_computation.8 | async-start | bytes 4866048 | tf_op jit(solution)/shard_map/all_gather | solution.py:138
  10.0 568.4 %reduce-scatter.18.cloned.1.call-start = ((), (), s32[]{:S(2)}) async-start(), calls=%async_computation.13 | async-start | bytes 405504
  62.1 87.0 %copy-start.43 = (bf16[128]{0:T(256)(128)(2,1)}, bf16[128]{0:T(256)(128)(2,1)S(1)}, u32[]{:S(2)}) copy-start(bf16[128]{0:T(256)(128)(2,1)S(1)} %get-tuple-element.283) | copy-start | bytes 772
  64.6 335.5 %copy-start.28 = (f32[768]{0:T(1024)}, f32[768]{0:T(1024)S(1)}, u32[]{:S(2)}) copy-start(f32[768]{0:T(1024)S(1)} %convert_element_type.110) | copy-start | bytes 9220
  64.7 195.5 %copy-start.39 = (f32[768]{0:T(1024)}, f32[768]{0:T(1024)S(1)}, u32[]{:S(2)}) copy-start(f32[768]{0:T(1024)S(1)} %convert_element_type.111) | copy-start | bytes 9220
  193.0 9.7 copy-start
  193.0 9.7 copy-start.3
  193.0 9.7 copy-start.19
  202.7 1.7 copy-start.9
  202.7 197.4 %copy-start.21 = (f32[1024]{0:T(1024)}, f32[1024]{0:T(1024)S(1)}, u32[]{:S(2)}) copy-start(f32[1024]{0:T(1024)S(1)} %broadcast_multiply_fusion.5) | copy-start | bytes 12292
  204.8 195.4 %copy-start.30 = (f32[1024]{0:T(1024)}, f32[1024]{0:T(1024)S(1)}, u32[]{:S(2)}) copy-start(f32[1024]{0:T(1024)S(1)} %add_rsqrt_fusion.1) | copy-start | bytes 12292
  204.8 55.4 %copy-start.41 = (f32[768]{0:T(1024)S(1)}, f32[768]{0:T(1024)}, u32[]{:S(2)}) copy-start(f32[768]{0:T(1024)} %convert_element_type.115) | copy-start | bytes 9220
  260.2 10.1 %copy-start.23 = (f32[768]{0:T(1024)S(1)}, f32[768]{0:T(1024)}, u32[]{:S(2)}) copy-start(f32[768]{0:T(1024)} %convert_element_type.116) | copy-start | bytes 9220
  260.2 10.1 %copy-start.32 = (f32[768]{0:T(1024)S(1)}, f32[768]{0:T(1024)}, u32[]{:S(2)}) copy-start(f32[768]{0:T(1024)} %convert_element_type.117) | copy-start | bytes 9220
  269.9 2.2 copy-start.18
  270.3 4.6 copy-start.44
  270.3 5.4 copy-start.45
  270.3 85.7 %copy-start.42 = (f32[128]{0:T(128)S(1)}, f32[128]{0:T(128)}, u32[]{:S(2)}) copy-start(f32[128]{0:T(128)} %convert_element_type.120) | copy-start | bytes 1540
  274.0 0.8 copy-start.12
  356.0 8.0 copy-start.24
  364.0 214.5 %reduce-scatter.10.cloned.1.call-start = ((), (), s32[]{:S(2)}) async-start(), calls=%async_computation.9 | async-start | bytes 2433024 | tf_op jit(solution)/shard_map/reduce_scatter | solution.py:283
  369.2 20.2 %copy-start.10 = (f32[1024,768]{0,1:T(8,128)S(1)}, f32[1024,768]{0,1:T(8,128)}, u32[]{:S(2)}) copy-start(f32[1024,768]{0,1:T(8,128)} %copy-done.9) | copy-start | bytes 9437188
  400.2 3.4 copy-start.46
  401.9 1.6 copy-start.14
  408.6 5.4 copy-start.1
  408.6 5.5 copy-start.4
  408.6 5.5 copy-start.20
  414.0 273.8 %reduce-scatter.16.cloned.1.call-start = ((), (), s32[]{:S(2)}) async-start(), calls=%async_computation.12 | async-start | bytes 7299072
  414.1 2.1 copy-start.6
  414.1 2.1 copy-start.7
  431.3 2.0 copy-start.8
  439.4 3.4 copy-start.2
  439.4 3.4 copy-start.5
  442.7 2.1 copy-start.6
  442.7 2.1 copy-start.7
  459.9 2.0 copy-start.8
  468.0 3.4 copy-start.2
  468.0 3.4 copy-start.5
  489.4 1.9 copy-start.15
  489.4 340.9 %reduce-scatter.14.cloned.1.call-start = ((), (), s32[]{:S(2)}) async-start(), calls=%async_computation.11 | async-start | bytes 9732096 | tf_op jit(solution)/shard_map/reduce_scatter | solution.py:289
  501.6 1.9 copy-start.11
  501.6 1.9 copy-start.22
  501.6 1.9 copy-start.29
  501.6 1.9 copy-start.31
  501.6 1.9 copy-start.40
  501.6 469.7 %reduce-scatter.12.cloned.1.call-start = ((), (), s32[]{:S(2)}) async-start(), calls=%async_computation.10 | async-start | bytes 9732096 | tf_op jit(solution)/shard_map/reduce_scatter | solution.py:287
  514.0 2.8 copy-start.25
  514.0 2.8 copy-start.13
  514.0 6.2 copy-start.26
  514.0 6.2 copy-start.27
  514.0 6.2 copy-start.33
  514.0 6.2 copy-start.35
  514.0 6.2 copy-start.36
  514.1 6.2 copy-start.37
  514.1 6.2 copy-start.38
Sparse Core Ops, SparseCore 0:
  10.8 63.2 all-gather.4
  76.9 52.7 all-gather.6
  132.5 62.5 all-gather.8
  197.8 62.3 all-gather.10
  364.1 94.5 reduce-scatter.17
  465.3 98.1 reduce-scatter.9
  569.7 118.0 reduce-scatter.15
  695.3 134.9 reduce-scatter.13
  836.8 134.4 reduce-scatter.11
where the time goes:
time: 983 us; the launch traced here: 978 us
  waiting for transfers between devices  413 us (42%)
  blocking collectives  236 us (24%)
  matrix products  191 us (19%)
  local copies, waits for them, and re-layouts  84 us (9%)
  other arithmetic  37.7 us (4%)
  between operations  14.8 us (2%)
    reduce_scatter x1, waiting for transfers between devices, shards(): lax.psum_scatter(outer_weight_grad, ('dp', 'fsdp'), scatter_dimension=0,...  142 us
    reduce_scatter x1, waiting for transfers between devices, shards(): lax.psum_scatter(inner_weight_grad, ('dp', 'fsdp'), scatter_dimension=0,...  141 us
    unnamed x11, waiting for transfers between devices  112 us
    unnamed x2, blocking collectives  84.4 us
    all_gather x1, blocking collectives, shards(): lax.all_gather(span_weight, ('dp', 'fsdp'), axis=0, tiled=True)  72.9 us
    dot_general x5, matrix products, matmul(): return jnp.dot(operand, matrix, preferred_element_type=jnp.float32)  61 us
    dot_general x5, matrix products, back_prod(): lax.dot_general(operand, matrix, (((1,), (1,)), ((), ())), preferred_elem...  45.6 us
    unnamed x123, local copies, waits for them, and re-layouts  41 us
  transfers between devices with their start and end apart: 9, of which 4 were waited for; matrix products, arithmetic and copies ran while one was open for 29% of the time, Pallas kernels for 0%

commit v1 on v0

--- a/solution.py
+++ b/solution.py
@@ -193,7 +193,7 @@
         jnp.where(member_query, jnp.exp(doc_flat[:, None] - local_peak[None, :]), 0.0), axis=0
     )
     peak_score = lax.pmax(local_peak, ("dp", "fsdp"))
-    mass_total = lax.psum(local_mass * jnp.exp(local_peak - peak_score), ("dp", "fsdp"))
+    mass_total = lax.psum(lax.psum(local_mass * jnp.exp(local_peak - peak_score), "fsdp"), "dp")
     marginal = peak_score + jnp.log(mass_total)
     likelihood = jnp.sum(marginal)
     gathered = (

time: 983 us -> 963 us (0.980)
  blocking collectives: 236 us -> 217 us
    psum x1 -> x2, blocking collectives: 39.5 us -> 22.1 us  [the longest x1 12 us: shards(): lax.psum(lax.psum(local_mass * jnp.exp(local_peak - peak_score), 'fsdp'),...]
where the time goes in v1:
time: 963 us; the launch traced here: 959 us
  waiting for transfers between devices  414 us (43%)
  blocking collectives  217 us (23%)
  matrix products  191 us (20%)
  local copies, waits for them, and re-layouts  84 us (9%)
  other arithmetic  37.7 us (4%)
  between operations  14.8 us (2%)
    reduce_scatter x1, waiting for transfers between devices, shards(): lax.psum_scatter(outer_weight_grad, ('dp', 'fsdp'), scatter_dimension=0,...  142 us
    reduce_scatter x1, waiting for transfers between devices, shards(): lax.psum_scatter(inner_weight_grad, ('dp', 'fsdp'), scatter_dimension=0,...  141 us
    unnamed x11, waiting for transfers between devices  113 us
    unnamed x2, blocking collectives  82.2 us
    all_gather x1, blocking collectives, shards(): lax.all_gather(span_weight, ('dp', 'fsdp'), axis=0, tiled=True)  72.9 us
    dot_general x5, matrix products, matmul(): return jnp.dot(operand, matrix, preferred_element_type=jnp.float32)  61.2 us
    dot_general x5, matrix products, back_prod(): lax.dot_general(operand, matrix, (((1,), (1,)), ((), ())), preferred_elem...  45.2 us
    unnamed x123, local copies, waits for them, and re-layouts  41 us
  transfers between devices with their start and end apart: 9, of which 4 were waited for; matrix products, arithmetic and copies ran while one was open for 29% of the time, Pallas kernels for 0%

profile of v1, /device:TPU:0, one launch (start us, length us, event | category | flops | bytes accessed | tf_op | source)
XLA Modules:
  0.0 958.9 jit_solution(8825059581699110310)
XLA Ops:
  19.5 42.6 %all-reduce.22 = (bf16[768]{0:T(1024)(128)(2,1)S(1)}, bf16[768]{0:T(1024)(128)(2,1)S(1)}, bf16[768]{0:T(1024)(128)(2,1)S(1)}, bf16[768]{0:T(1024)(128)(2,1)S(1)}...) all-reduce(bf16[768]{0:T(1024)(128)(2,1)S(1)} %dynamic-update-slice, ...), channel_id=1, replica_groups=mesh['dp'=8,'fsdp'=4] {'dp','fsdp'}, use_global_device_ids=true, to_apply=%add.1 | all-reduce | flops 9344 | bytes 37376
  62.1 2.6 copy.106
  66.5 72.9 %all_gather.66 = bf16[768,128]{1,0:T(8,128)(2,1)} all-gather(bf16[24,128]{1,0:T(8,128)(2,1)S(1)} %copy-done.34), channel_id=1, replica_groups=mesh['dp'=8,'fsdp'=4] {'dp','fsdp'}, dimensions={0}, use_global_device_ids=true | all-gather | bytes 202752 | tf_op jit(solution)/shard_map/all_gather | solution.py:142
  139.9 1.6 copy.113
  141.6 7.5 add_convert_fusion.1
  149.1 6.6 copy.107
  155.7 8.9 reshape.253
  164.6 5.4 slice_bitcast_fusion
  172.1 20.9 %while.22 = (s32[]{:T(128)}, bf16[2,512,12,64]{1,3,2,0:T(8,128)(2,1)}, f32[2,12,512,1]{2,1,3,0:T(8,128)S(1)}, bf16[2,512,12,64]{1,3,2,0:T(8,128)(2,1)}, s32[2,51...) while((s32[]{:T(128)}, ...), condition=%wide.region_5.6_spmd, body=%wide.region_2.5_spmd.sunk | while | flops 843704320 | bytes 42172508 | solution.py:169
  172.3 2.1 fusion.124
  174.4 2.6 fusion.125
  177.0 5.5 fusion.126
  182.7 2.1 fusion.124
  184.8 2.6 fusion.125
  187.3 5.5 fusion.126
  193.0 4.2 copy.111
  197.2 1.6 copy.159
  198.8 3.9 fusion.79
  202.8 1.6 copy-done.9
  204.8 37.9 %multiply_convert_fusion.1 = (bf16[1024,3072]{1,0:T(8,128)(2,1)}, f32[1024,3072]{1,0:T(8,128)}, f32[1024,3072]{1,0:T(8,128)}) fusion(f32[3072]{0:T(1024)S(1)} %convert_element_type.113, bf16[768,3072]{1,0:T(8,128)(2,1)} %all-gather.9.cloned.1.call-done, f32[1024,768]{0,1:T(8,128)} %copy-done.9, f32[768]{0:T(1024)S(1)} %convert_element_type.111, ...), kind=kOutput, calls=%fused_computation.64 | convolution fusion | flops 5043388416 | bytes 39348224 | tf_op jit(solution)/shard_map/dot_general | solution.py:16
  242.7 17.4 %all-gather.11.cloned.1.call-done = bf16[3072,768]{1,0:T(8,128)(2,1)} async-done(((bf16[96,768]{1,0:T(8,128)(2,1)}), bf16[3072,768]{1,0:T(8,128)(2,1)}) %all-gather.11.cloned.1.call-update) | async-done | bytes 4718608 | tf_op jit(solution)/shard_map/all_gather | solution.py:138
  260.2 9.9 %fusion.80 = (f32[1024]{0:T(1024)S(1)}, f32[1024,768]{0,1:T(8,128)S(1)}) fusion(f32[768]{0:T(1024)S(1)} %copy-done.41, bf16[1024,3072]{1,0:T(8,128)(2,1)} %get-tuple-element.292, bf16[3072,768]{1,0:T(8,128)(2,1)} %all-gather.11.cloned.1.call-done, f32[768]{0:T(1024)S(1)} %convert_element_type.111, f32[768]{0:T(1024)S(1)} %convert_element_type.110, ...), kind=kOutput, calls=%fused_computation.156 | convolution fusion | flops 4837342208 | bytes 17323008 | tf_op jit(solution)/shard_map/dot_general | solution.py:16
  270.5 1.7 add_convert_fusion.2
  272.2 2.0 fusion.81
  276.0 39.6 %pmax.7 = f32[64]{0:T(128)S(1)} all-reduce(f32[64]{0:T(128)S(1)} %select_reduce_fusion.4), channel_id=1, replica_groups=mesh['dp'=8,'fsdp'=4] {'dp','fsdp'}, use_global_device_ids=true, to_apply=%region_13.14 | all-reduce | flops 64 | bytes 512 | tf_op jit(solution)/shard_map/pmax | solution.py:195
  315.6 10.1 %psum.14 = f32[64]{0:T(128)S(1)} all-reduce(f32[64]{0:T(128)S(1)} %exponential_multiply_fusion), channel_id=1, replica_groups=mesh['dp'=8,'fsdp'=4] {'fsdp'}, use_global_device_ids=true, to_apply=%region_15.16 | all-reduce | flops 64 | bytes 512 | tf_op jit(solution)/shard_map/psum | solution.py:196
  325.7 12.0 %psum.15 = f32[64]{0:T(128)S(1)} all-reduce(f32[64]{0:T(128)S(1)} %psum.14), channel_id=1, replica_groups=mesh['dp'=8,'fsdp'=4] {'dp'}, use_global_device_ids=true, to_apply=%region_16.17 | all-reduce | flops 64 | bytes 512 | tf_op jit(solution)/shard_map/psum | solution.py:196
  338.7 2.8 fusion.54
  341.6 5.1 multiply_reduce_fusion.1
  346.8 5.2 convert_reduce_fusion.2
  352.0 19.7 %convert_reduce_fusion = (f32[3072]{0:T(1024)}, bf16[1024,3072]{1,0:T(8,128)(2,1)}) fusion(f32[1024,3072]{1,0:T(8,128)} %get-tuple-element.293, bf16[3072,768]{1,0:T(8,128)(2,1)} %all-gather.11.cloned.1.call-done, f32[1024,768]{0,1:T(8,128)} %get-tuple-element.285, f32[1024,3072]{1,0:T(8,128)} %get-tuple-element.305, f32[3072]{0:T(1024)S(1)} %convert_element_type.113), kind=kOutput, calls=%fused_computation.62 | convolution fusion | flops 4886098944 | bytes 39346176 | tf_op jit(solution)/shard_map/dot_general | solution.py:26
  371.7 10.8 %multiply_reduce_fusion.2 = (f32[768]{0:T(1024)}, f32[1024]{0:T(1024)S(1)}, f32[1024]{0:T(1024)S(1)}, f32[768]{0:T(1024)}, f32[1024,768]{0,1:T(8,128)S(1)}) fusion(f32[1024,768]{0,1:T(8,128)S(1)} %copy-done.10, f32[1024]{0:T(1024)S(1)} %add_rsqrt_fusion.1, f32[1024]{0:T(1024)S(1)} %broadcast_multiply_fusion.5, f32[768]{0:T(1024)S(1)} %convert_element_type.110, ...), kind=kOutput, calls=%fused_computation.83 | convolution fusion | flops 4839698432 | bytes 20472832 | tf_op jit(solution)/shard_map/dot_general | solution.py:26
  382.5 1.7 convert_reduce_fusion.3
  384.2 1.6 copy-done.14
  390.9 5.4 fusion.64
  396.5 57.5 %while.23 = (s32[]{:T(128)}, bf16[2,512,2304]{2,1,0:T(8,128)(2,1)}, bf16[2,512,12,64]{1,3,2,0:T(8,128)(2,1)S(1)}, s32[2,512]{1,0:T(2,128)S(1)}, bf16[2,512,12,64...) while((s32[]{:T(128)}, bf16[2,512,2304]{2,1,0:T(8,128)(2,1)}, ...), condition=%wide.region_26.27_spmd, body=%wide.region_24.26_spmd.sunk | while | flops 2064640000 | bytes 149095184 | solution.py:270
  396.5 1.8 fusion.135
  398.6 6.9 multiply_reduce_fusion.10
  405.5 7.0 multiply_convert_fusion.6
  413.7 2.0 multiply_bitcast_fusion.4
  415.7 3.2 fusion.136
  419.2 2.6 copy.163
  421.7 3.4 constant_dynamic-update-slice_fusion.2
  425.1 1.8 fusion.135
  427.2 6.9 multiply_reduce_fusion.10
  434.1 7.0 multiply_convert_fusion.6
  442.3 2.0 multiply_bitcast_fusion.4
  444.3 3.2 fusion.136
  447.8 2.6 copy.163
  450.3 3.4 constant_dynamic-update-slice_fusion.2
  454.0 9.7 %convolution_bitcast_fusion = f32[768,2304]{0,1:T(8,128)} fusion(bf16[1024,2304]{1,0:T(8,128)(2,1)} %bitcast.163, bf16[1024,768]{1,0:T(8,128)(2,1)} %param.23), kind=kOutput, calls=%fused_computation.80 | convolution fusion | flops 3623878656 | bytes 13369344 | tf_op jit(solution)/shard_map/dot_general | solution.py:20
  463.7 8.1 copy.134
  471.9 1.9 copy-done.15
  473.7 10.2 %fusion.67 = f32[3072,768]{1,0:T(8,128)} fusion(bf16[1024,3072]{1,0:T(8,128)(2,1)} %get-tuple-element.292, f32[1024,768]{0,1:T(8,128)S(1)} %copy-done.15), kind=kOutput, calls=%fused_computation.147 | convolution fusion | flops 4832624640 | bytes 18874368 | tf_op jit(solution)/shard_map/dot_general | solution.py:20
  484.1 1.8 copy-done.11
  485.9 10.5 %fusion.71 = f32[768,3072]{1,0:T(8,128)} fusion(bf16[1024,3072]{1,0:T(8,128)(2,1)} %get-tuple-element.311, f32[1024,768]{0,1:T(8,128)S(1)} %copy-done.11, f32[768]{0:T(1024)S(1)} %copy-done.40, f32[768]{0:T(1024)S(1)} %copy-done.29, f32[1024]{0:T(1024)S(1)} %copy-done.31, f32[1024]{0:T(1024)S(1)} %copy-done.22), kind=kOutput, calls=%fused_computation.151 | convolution fusion | flops 4835770368 | bytes 18888704 | tf_op jit(solution)/shard_map/dot_general | solution.py:20
  496.4 2.7 copy.123
  499.5 3.1 convert_reduce_fusion.1
  502.6 39.6 %all-reduce.21 = (f32[768]{0:T(1024)S(1)}, f32[768]{0:T(1024)S(1)}, f32[768]{0:T(1024)S(1)}, f32[768]{0:T(1024)S(1)}, f32[768]{0:T(1024)S(1)}, /*index=5*/f32[30...) all-reduce(f32[768]{0:T(1024)S(1)} %get-tuple-element.302, ...), channel_id=3, replica_groups=mesh['dp'=8,'fsdp'=4] {'dp','fsdp'}, use_global_device_ids=true, to_apply=%region_29.30.clone | all-reduce | flops 9344 | bytes 74752
  546.9 8.1 convolution_add_fusion.1
  555.0 2.4 copy.124
  558.5 110.1 %reduce-scatter.16.cloned.1.call-done = f32[24,2304]{1,0:T(8,128)} async-done(((f32[768,2304]{1,0:T(8,128)}), f32[24,2304]{1,0:T(8,128)}) %reduce-scatter.16.cloned.1.call-update) | async-done | bytes 221200
  668.7 142.2 %reduce-scatter.14.cloned.1.call-done = f32[96,768]{1,0:T(8,128)} async-done(((f32[3072,768]{1,0:T(8,128)}), f32[96,768]{1,0:T(8,128)}) %reduce-scatter.14.cloned.1.call-update) | async-done | bytes 294928 | tf_op jit(solution)/shard_map/reduce_scatter | solution.py:289
  810.9 141.2 %reduce-scatter.12.cloned.1.call-done = f32[24,3072]{1,0:T(8,128)} async-done(((f32[768,3072]{1,0:T(8,128)}), f32[24,3072]{1,0:T(8,128)}) %reduce-scatter.12.cloned.1.call-update) | async-done | bytes 294928 | tf_op jit(solution)/shard_map/reduce_scatter | solution.py:287
  (221 shorter events, 35.6 us)
Async XLA Ops:
  7.2 59.3 %copy-start.34 = (bf16[24,128]{1,0:T(8,128)(2,1)S(1)}, bf16[24,128]{1,0:T(8,128)(2,1)}, u32[]{:S(2)}) copy-start(bf16[24,128]{1,0:T(8,128)(2,1)} %param.40) | copy-start | bytes 18436
  7.2 132.7 %copy-start.16 = (bf16[1024,768]{1,0:T(8,128)(2,1)S(1)}, bf16[1024,768]{1,0:T(8,128)(2,1)}, u32[]{:S(2)}) copy-start(bf16[1024,768]{1,0:T(8,128)(2,1)} %param.24) | copy-start | bytes 4718596
  7.2 134.3 %all-gather.5.cloned.1.call-start = ((), (), s32[]{:S(2)}) async-start(), calls=%async_computation.5 | async-start | bytes 3649536 | tf_op jit(solution)/shard_map/all_gather | solution.py:129
  7.9 133.6 %copy-start.17 = (bf16[1024,768]{1,0:T(8,128)(2,1)S(1)}, bf16[1024,768]{1,0:T(8,128)(2,1)}, u32[]{:S(2)}) copy-start(bf16[1024,768]{1,0:T(8,128)(2,1)} %param.23) | copy-start | bytes 4718596
  8.0 190.8 %all-gather.7.cloned.1.call-start = ((), (), s32[]{:S(2)}) async-start(), calls=%async_computation.6 | async-start | bytes 1216512 | tf_op jit(solution)/shard_map/all_gather | solution.py:132
  8.7 196.1 %all-gather.9.cloned.1.call-start = ((), (), s32[]{:S(2)}) async-start(), calls=%async_computation.7 | async-start | bytes 4866048 | tf_op jit(solution)/shard_map/all_gather | solution.py:136
  9.4 250.7 %all-gather.11.cloned.1.call-start = ((), (), s32[]{:S(2)}) async-start(), calls=%async_computation.8 | async-start | bytes 4866048 | tf_op jit(solution)/shard_map/all_gather | solution.py:138
  10.0 548.5 %reduce-scatter.18.cloned.1.call-start = ((), (), s32[]{:S(2)}) async-start(), calls=%async_computation.13 | async-start | bytes 405504
  62.1 87.0 %copy-start.43 = (bf16[128]{0:T(256)(128)(2,1)}, bf16[128]{0:T(256)(128)(2,1)S(1)}, u32[]{:S(2)}) copy-start(bf16[128]{0:T(256)(128)(2,1)S(1)} %get-tuple-element.283) | copy-start | bytes 772
  64.6 317.8 %copy-start.28 = (f32[768]{0:T(1024)}, f32[768]{0:T(1024)S(1)}, u32[]{:S(2)}) copy-start(f32[768]{0:T(1024)S(1)} %convert_element_type.110) | copy-start | bytes 9220
  64.7 195.5 %copy-start.39 = (f32[768]{0:T(1024)}, f32[768]{0:T(1024)S(1)}, u32[]{:S(2)}) copy-start(f32[768]{0:T(1024)S(1)} %convert_element_type.111) | copy-start | bytes 9220
  193.0 9.7 %copy-start = (bf16[2,512,12,64]{1,3,2,0:T(8,128)(2,1)}, bf16[2,512,12,64]{1,3,2,0:T(8,128)(2,1)S(1)}, u32[]{:S(2)}) copy-start(bf16[2,512,12,64]{1,3,2,0:T(8,128)(2,1)S(1)} %get-tuple-element.474) | copy-start | bytes 4718596
  193.0 9.7 %copy-start.3 = (bf16[2,512,12,64]{1,3,2,0:T(8,128)(2,1)}, bf16[2,512,12,64]{1,3,2,0:T(8,128)(2,1)S(1)}, u32[]{:S(2)}) copy-start(bf16[2,512,12,64]{1,3,2,0:T(8,128)(2,1)S(1)} %get-tuple-element.485) | copy-start | bytes 4718596
  193.0 9.7 %copy-start.19 = (f32[2,12,512,1]{2,1,3,0:T(8,128)}, f32[2,12,512,1]{2,1,3,0:T(8,128)S(1)}, u32[]{:S(2)}) copy-start(f32[2,12,512,1]{2,1,3,0:T(8,128)S(1)} %get-tuple-element.443) | copy-start | bytes 147460
  202.7 1.7 copy-start.9
  202.7 179.7 %copy-start.21 = (f32[1024]{0:T(1024)}, f32[1024]{0:T(1024)S(1)}, u32[]{:S(2)}) copy-start(f32[1024]{0:T(1024)S(1)} %broadcast_multiply_fusion.5) | copy-start | bytes 12292
  204.8 177.7 %copy-start.30 = (f32[1024]{0:T(1024)}, f32[1024]{0:T(1024)S(1)}, u32[]{:S(2)}) copy-start(f32[1024]{0:T(1024)S(1)} %add_rsqrt_fusion.1) | copy-start | bytes 12292
  204.8 55.4 %copy-start.41 = (f32[768]{0:T(1024)S(1)}, f32[768]{0:T(1024)}, u32[]{:S(2)}) copy-start(f32[768]{0:T(1024)} %convert_element_type.115) | copy-start | bytes 9220
  260.2 10.3 %copy-start.23 = (f32[768]{0:T(1024)S(1)}, f32[768]{0:T(1024)}, u32[]{:S(2)}) copy-start(f32[768]{0:T(1024)} %convert_element_type.116) | copy-start | bytes 9220
  260.2 10.3 %copy-start.32 = (f32[768]{0:T(1024)S(1)}, f32[768]{0:T(1024)}, u32[]{:S(2)}) copy-start(f32[768]{0:T(1024)} %convert_element_type.117) | copy-start | bytes 9220
  270.1 2.2 copy-start.18
  270.5 4.6 copy-start.44
  270.5 5.4 copy-start.45
  270.5 68.2 %copy-start.42 = (f32[128]{0:T(128)S(1)}, f32[128]{0:T(128)}, u32[]{:S(2)}) copy-start(f32[128]{0:T(128)} %convert_element_type.120) | copy-start | bytes 1540
  274.2 0.8 copy-start.12
  338.7 8.0 copy-start.24
  346.7 211.8 %reduce-scatter.10.cloned.1.call-start = ((), (), s32[]{:S(2)}) async-start(), calls=%async_computation.9 | async-start | bytes 2433024 | tf_op jit(solution)/shard_map/reduce_scatter | solution.py:283
  352.0 19.7 %copy-start.10 = (f32[1024,768]{0,1:T(8,128)S(1)}, f32[1024,768]{0,1:T(8,128)}, u32[]{:S(2)}) copy-start(f32[1024,768]{0,1:T(8,128)} %copy-done.9) | copy-start | bytes 9437188
  382.5 3.4 copy-start.46
  384.2 1.6 copy-start.14
  390.9 5.5 copy-start.1
  390.9 5.5 copy-start.4
  390.9 5.5 copy-start.20
  396.4 272.3 %reduce-scatter.16.cloned.1.call-start = ((), (), s32[]{:S(2)}) async-start(), calls=%async_computation.12 | async-start | bytes 7299072
  396.5 2.1 copy-start.6
  396.5 2.1 copy-start.7
  413.7 2.0 copy-start.8
  421.7 3.4 copy-start.2
  421.7 3.4 copy-start.5
  425.1 2.1 copy-start.6
  425.1 2.1 copy-start.7
  442.3 2.0 copy-start.8
  450.3 3.4 copy-start.2
  450.3 3.4 copy-start.5
  471.8 1.9 copy-start.15
  471.8 339.1 %reduce-scatter.14.cloned.1.call-start = ((), (), s32[]{:S(2)}) async-start(), calls=%async_computation.11 | async-start | bytes 9732096 | tf_op jit(solution)/shard_map/reduce_scatter | solution.py:289
  484.0 1.9 copy-start.11
  484.0 1.9 copy-start.22
  484.0 1.9 copy-start.29
  484.0 1.9 copy-start.31
  484.0 1.9 copy-start.40
  484.0 468.1 %reduce-scatter.12.cloned.1.call-start = ((), (), s32[]{:S(2)}) async-start(), calls=%async_computation.10 | async-start | bytes 9732096 | tf_op jit(solution)/shard_map/reduce_scatter | solution.py:287
  496.3 2.8 copy-start.25
  496.3 2.8 copy-start.13
  496.4 6.2 copy-start.26
  496.4 6.2 copy-start.27
  496.4 6.2 copy-start.33
  496.4 6.2 copy-start.35
  496.4 6.2 copy-start.36
  496.4 6.2 copy-start.37
  496.4 6.2 copy-start.38
Sparse Core Ops, SparseCore 0:
  10.8 63.2 all-gather.4
  76.9 52.7 all-gather.6
  132.5 62.5 all-gather.8
  197.8 62.3 all-gather.10
  346.8 92.6 reduce-scatter.17
  446.0 98.1 reduce-scatter.9
  550.5 118.1 reduce-scatter.15
  676.2 134.7 reduce-scatter.13
  817.4 134.6 reduce-scatter.11
